TPU v7x, 32 devices: a whole 2x2x4 slice. The times are simulated.
32 devices in a mesh: group: 2 (over y), seq: 4 (over z), blk: 2 (over x), tp: 2 (over core).
Axes of the slice: x: 2, y: 2, z: 4, core: 2. Of those that a mesh axis runs over, the one named last changes fastest.
Arguments:
- tokens: bfloat16 [2048, 3072], P(('group', 'blk'), ('seq', 'tp')), parts along dimension 0, may hold values from -64 to 64
- timestep: int32 [2], P('group'), parts along dimension 0, may hold values from 25 to 49
- padded_heads: int32 [2], P('group'), parts along dimension 0, may hold values from 1 to 3
- modulation: float32 [50, 3, 3072], replicated, may hold values from -3 to 3
- qkv_weight: bfloat16 [3, 3072, 1024], P(None, 'blk', ('seq', 'tp')), may hold values from -1 to 1
- out_weight: bfloat16 [1024, 3072], P(('seq', 'tp'), 'blk'), may hold values from -0.5 to 0.5
Outputs:
- update: bfloat16 [2048, 3072], P(('group', 'blk'), ('seq', 'tp')), parts along dimension 0
There are 2 independent parts, one for each index of `group`. A program takes and returns all parts, laid end to end along the dimension named above; an argument that names none is the same for every part. Nothing has to cross between parts.
All inputs are finite; a program needn't handle non-finite values.
Results may differ from a plain program's by a relative error of at most 0.023.
Values may be sent and summed in bfloat16 or wider, within the bound.
A program may use at most 64 MiB of HBM per device.

v0:
```python
import math
import jax
import jax.numpy as jnp
from jax import lax
from jax.sharding import PartitionSpec as P

epsilon = 1e-06
neg_large = -1e30


def collect(own_part):
    gathered = lax.all_gather(own_part, ("seq", "tp"), axis=1, tiled=True)
    return gathered


def attend_block(running, queries, key_block, value_block, factor):
    largest, totals, weighted = running
    scores = (
        lax.dot_general(
            queries, key_block, (((1,), (1,)), ((), ())), preferred_element_type=jnp.float32
        )
        * factor
    )
    new_max = jnp.maximum(largest, jnp.max(scores, axis=1))
    rescale = jnp.exp(largest - new_max)
    weights = jnp.exp(scores - new_max[:, None])
    totals = totals * rescale + jnp.sum(weights, axis=1)
    weighted = weighted * rescale[:, None] + jnp.dot(
        weights.astype(jnp.bfloat16), value_block, preferred_element_type=jnp.float32
    )
    return (new_max, totals, weighted)


def body(tokens, timestep, padded_heads, modulation, qkv_weight, out_weight):
    slices = lax.axis_size(("seq", "tp"))
    own_index = lax.axis_index(("seq", "tp"))
    model_width = modulation.shape[2]
    own_width = model_width // slices
    token_rows = tokens.shape[0]
    head_size = out_weight.shape[0]
    table_row = lax.dynamic_index_in_dim(modulation, timestep[0], 0, keepdims=False)
    own_entry = lax.dynamic_slice_in_dim(table_row, own_index * own_width, own_width, 1)
    gathered = collect(tokens).astype(jnp.float32)
    average = jnp.mean(gathered, axis=1, keepdims=True)
    centered = gathered - average
    spread = jnp.mean(centered * centered, axis=1, keepdims=True)
    normed = centered * lax.rsqrt(spread + epsilon)
    modulated = (normed * (1.0 + table_row[1]) + table_row[0]).astype(jnp.bfloat16)
    projected = jnp.einsum(
        "td,kde->kte",
        modulated,
        lax.all_gather(qkv_weight, "blk", axis=1, tiled=True),
        preferred_element_type=jnp.float32,
    ).astype(jnp.bfloat16)
    queries = projected[0]
    factor = 1.0 / math.sqrt(head_size)
    initial = (
        jnp.full((token_rows,), neg_large, jnp.float32),
        jnp.zeros((token_rows,), jnp.float32),
        jnp.zeros((token_rows, head_size), jnp.float32),
    )
    key_piece = lax.all_gather(projected[1], "blk", axis=0, tiled=True)
    value_piece = lax.all_gather(projected[2], "blk", axis=0, tiled=True)
    length = key_piece.shape[0]

    def one_block(counter, inner_state):
        key_block = lax.dynamic_slice_in_dim(key_piece, counter * 512, 512, 0)
        value_block = lax.dynamic_slice_in_dim(value_piece, counter * 512, 512, 0)
        return attend_block(inner_state, queries, key_block, value_block, factor)

    largest, exp_totals, weighted = lax.fori_loop(0, length // 512, one_block, initial)
    attended = weighted / exp_totals[:, None]
    live_heads = slices - padded_heads[0]
    masked = jnp.where(own_index < live_heads, attended, 0.0).astype(jnp.bfloat16)
    head_term = jnp.dot(
        masked,
        lax.all_gather(out_weight, "blk", axis=1, tiled=True),
        preferred_element_type=jnp.float32,
    )
    summed = lax.psum_scatter(
        head_term.astype(jnp.bfloat16), ("seq", "tp"), scatter_dimension=1, tiled=True
    ).astype(jnp.float32)
    return (own_entry[2] * summed).astype(jnp.bfloat16)


def solution(mesh):
    return jax.shard_map(
        body,
        mesh=mesh,
        in_specs=(
            P(("group", "blk"), ("seq", "tp")),
            P("group"),
            P("group"),
            P(),
            P(None, "blk", ("seq", "tp")),
            P(("seq", "tp"), "blk"),
        ),
        out_specs=P(("group", "blk"), ("seq", "tp")),
        check_vma=False,
    )
```

profile of v0, /device:TPU:0, one launch (start us, length us, event | category | flops | bytes accessed | tf_op | source)
XLA Modules:
  0.0 157.3 jit_solution(16973399973763437814)
XLA Ops:
  6.5 0.0 all-gather.5.cloned.1.call-start
  6.5 0.7 all-gather.5.cloned.1.call-update
  7.3 0.0 all-gather.7.cloned.1.call-start
  7.3 0.7 all-gather.7.cloned.1.call-update
  8.0 0.0 reduce-scatter.4.cloned.1.call-start
  9.4 14.8 %all_gather.19 = bf16[128,3072]{1,0:T(8,128)(2,1)} all-gather(bf16[128,1536]{1,0:T(8,128)(2,1)} %param.13), channel_id=1, replica_groups=mesh['group'=2,'seq'=4,'blk'=2,'tp'=2] {'blk'}, dimensions={1}, use_global_device_ids=true | all-gather | bytes 1179648 | tf_op jit(solution)/shard_map/all_gather | solution.py:77
  24.1 1.0 dynamic-slice_add_fusion
  25.1 24.4 %all-gather.5.cloned.1.call-done = bf16[512,3072]{1,0:T(8,128)(2,1)} async-done(((bf16[512,384]{1,0:T(8,128)(2,1)}), bf16[512,3072]{1,0:T(8,128)(2,1)}) %all-gather.5.cloned.1.call-update) | async-done | bytes 3145744 | tf_op jit(solution)/shard_map/all_gather | solution.py:12
  49.5 0.0 copy-start
  49.5 2.5 %convert_reduce_fusion = f32[512]{0:T(512)S(1)} fusion(bf16[512,3072]{1,0:T(8,128)(2,1)} %all-gather.5.cloned.1.call-done), kind=kLoop, calls=%fused_computation.16 | loop fusion | flops 3145216 | bytes 3147776 | tf_op jit(solution)/shard_map/reduce_sum | solution.py:44
  52.0 0.3 copy-done
  52.3 1.0 fusion.11
  53.3 33.1 %all-gather.7.cloned.1.call-done = bf16[3,3072,128]{2,1,0:T(8,128)(2,1)} async-done(((bf16[3,1536,128]{2,1,0:T(8,128)(2,1)}), bf16[3,3072,128]{2,1,0:T(8,128)(2,1)}) %all-gather.7.cloned.1.call-update) | async-done | bytes 2359312 | tf_op jit(solution)/shard_map/all_gather | solution.py:52
  86.4 3.5 %fusion.21 = bf16[3,512,128]{2,1,0:T(8,128)(2,1)S(1)} fusion(bf16[3,3072,128]{2,1,0:T(8,128)(2,1)} %all-gather.7.cloned.1.call-done, bf16[512,3072]{1,0:T(8,128)(2,1)S(1)} %copy-done, f32[3072]{0:T(1024)S(1)} %bitcast.32, f32[3072]{0:T(1024)S(1)} %bitcast.31, f32[512]{0:T(512)S(1)} %add_rsqrt_fusion, f32[512]{0:T(512)S(1)} %broadcast_multiply_fusion), kind=kOutput, calls=%fused_computation.27 | convolution fusion | flops 1217593344 | bytes 5926912 | tf_op jit(solution)/shard_map/td,kde->kte/dot_general | solution.py:49
  90.0 5.7 %all-gather = bf16[1,1024,128]{2,1,0:T(8,128)(2,1)S(1)} all-gather(bf16[1,512,128]{2,1,0:T(8,128)(2,1)S(1)} %get-tuple-element.178), channel_id=2, replica_groups=mesh['group'=2,'seq'=4,'blk'=2,'tp'=2] {'blk'}, dimensions={1}, use_global_device_ids=true | all-gather | bytes 393216 | tf_op jit(solution)/shard_map/all_gather | solution.py:62
  95.7 5.6 %all-gather.1 = bf16[1,1024,128]{2,1,0:T(8,128)(2,1)S(1)} all-gather(bf16[1,512,128]{2,1,0:T(8,128)(2,1)S(1)} %get-tuple-element.176), channel_id=3, replica_groups=mesh['group'=2,'seq'=4,'blk'=2,'tp'=2] {'blk'}, dimensions={1}, use_global_device_ids=true | all-gather | bytes 393216 | tf_op jit(solution)/shard_map/all_gather | solution.py:63
  101.3 1.9 %while.18 = (s32[]{:T(128)}, f32[512]{0:T(512)S(1)}, f32[512]{0:T(512)S(1)}, f32[512,128]{1,0:T(8,128)S(1)}, bf16[1024,128]{1,0:T(8,128)(2,1)S(1)}, /*index=5*/b...) while((s32[]{:T(128)}, f32[512]{0:T(512)S(1)}, ...), condition=%wide.region_5.6_spmd.clone, body=%wide.region_2.5_spmd.clone.sunk | while | flops 135989760 | bytes 4096175 | solution.py:71
  101.3 0.3 fusion.42
  101.7 0.2 fusion.43
  101.9 0.4 convolution_add_fusion.2
  102.3 0.3 fusion.42
  102.6 0.2 fusion.43
  102.8 0.4 convolution_add_fusion.2
  103.2 2.2 %convolution_convert_fusion = bf16[512,3072]{1,0:T(8,128)(2,1)S(1)} fusion(bf16[128,3072]{1,0:T(8,128)(2,1)} %all_gather.19, f32[512,128]{1,0:T(8,128)S(1)} %get-tuple-element.130, f32[512]{0:T(512)S(1)} %get-tuple-element.131, pred[]{:T(512)S(6)} %lt.25), kind=kOutput, calls=%fused_computation.23 | convolution fusion | flops 404422656 | bytes 4196353 | tf_op jit(solution)/shard_map/dot_general | solution.py:75
  105.4 2.8 %copy.7 = bf16[512,3072]{0,1:T(8,128)(2,1)} copy(bf16[512,3072]{1,0:T(8,128)(2,1)S(1)} %convolution_convert_fusion) | data formatting | bytes 6291456
  108.2 0.0 reduce-scatter.4.cloned.1.call-update
  108.3 0.8 dynamic-slice_reduce_fusion
  109.1 39.7 %reduce-scatter.4.cloned.1.call-done = bf16[384,512]{1,0:T(8,128)(2,1)} async-done(((bf16[3072,512]{1,0:T(8,128)(2,1)}), bf16[384,512]{1,0:T(8,128)(2,1)}) %reduce-scatter.4.cloned.1.call-update) | async-done | bytes 393232
  148.8 1.2 copy.8
  150.0 0.8 multiply_convert_fusion
  (12 shorter events, 0.1 us)
Async XLA Ops:
  6.5 42.9 %all-gather.5.cloned.1.call-start = ((), (), s32[]{:S(2)}) async-start(), calls=%async_computation.1 | async-start | bytes 3538944 | tf_op jit(solution)/shard_map/all_gather | solution.py:12
  7.3 79.2 %all-gather.7.cloned.1.call-start = ((), (), s32[]{:S(2)}) async-start(), calls=%async_computation.2 | async-start | bytes 3538944 | tf_op jit(solution)/shard_map/all_gather | solution.py:52
  8.0 140.8 %reduce-scatter.4.cloned.1.call-start = ((), (), s32[]{:S(2)}) async-start(), calls=%async_computation.3 | async-start | bytes 3538944
  49.5 2.8 %copy-start = (bf16[512,3072]{1,0:T(8,128)(2,1)S(1)}, bf16[512,3072]{1,0:T(8,128)(2,1)}, u32[]{:S(2)}) copy-start(bf16[512,3072]{1,0:T(8,128)(2,1)} %all-gather.5.cloned.1.call-done) | copy-start | bytes 9437188
Sparse Core Ops, SparseCore 0:
  8.9 40.4 all-gather.4
  51.0 35.3 all-gather.6
  108.4 40.3 reduce-scatter.3
where the time goes:
time: 158 us; the launch traced here: 157 us
  waiting for transfers between devices  98.6 us (62%)
  blocking collectives  26.1 us (17%)
  between operations  14.5 us (9%)
  matrix products  7.03 us (4%)
  other arithmetic  5.73 us (4%)
  local copies, waits for them, and re-layouts  5.18 us (3%)
    unnamed x4, waiting for transfers between devices  41.1 us
    all_gather x1, waiting for transfers between devices, body(): lax.all_gather(qkv_weight, 'blk', axis=1, tiled=True)  33.1 us
    all_gather x1, waiting for transfers between devices, collect(): gathered = lax.all_gather(own_part, ('seq', 'tp'), axis=1, tiled=True)  24.4 us
    all_gather x1, blocking collectives, body(): lax.all_gather(out_weight, 'blk', axis=1, tiled=True)  14.8 us
    all_gather x1, blocking collectives, body(): key_piece = lax.all_gather(projected[1], 'blk', axis=0, tiled=True)  5.73 us
    all_gather x1, blocking collectives, body(): value_piece = lax.all_gather(projected[2], 'blk', axis=0, tiled=True)  5.62 us
    unnamed x4, local copies, waits for them, and re-layouts  4.33 us
    dot_general x1, matrix products, body(): jnp.einsum('td,kde->kte', modulated, lax.all_gather(qkv_weight, 'blk', ax...  3.52 us
  transfers between devices with their start and end apart: 3, of which 3 were waited for; matrix products, arithmetic and copies ran while one was open for 3% of the time, Pallas kernels for 0%

commit v1 on v0

--- a/solution.py
+++ b/solution.py
@@ -6,6 +6,18 @@
 
 epsilon = 1e-06
 neg_large = -1e30
+
+
+def product_in_turn(x, axis, dim, product):
+    size, position, rows = (lax.axis_size(axis), lax.axis_index(axis), x.shape[dim])
+    right = [(i, (i + 1) % size) for i in range(size)]
+    current, total = (x, None)
+    for hop in range(size):
+        upcoming = lax.ppermute(current, axis, right) if hop < size - 1 else None
+        take_in = product(current, (position - hop) % size * rows)
+        total = take_in if total is None else total + take_in
+        current = upcoming
+    return total
 
 
 def collect(own_part):
@@ -46,11 +58,16 @@
     spread = jnp.mean(centered * centered, axis=1, keepdims=True)
     normed = centered * lax.rsqrt(spread + epsilon)
     modulated = (normed * (1.0 + table_row[1]) + table_row[0]).astype(jnp.bfloat16)
-    projected = jnp.einsum(
-        "td,kde->kte",
-        modulated,
-        lax.all_gather(qkv_weight, "blk", axis=1, tiled=True),
-        preferred_element_type=jnp.float32,
+    projected = product_in_turn(
+        qkv_weight,
+        "blk",
+        1,
+        lambda own_block, start: jnp.einsum(
+            "td,kde->kte",
+            lax.dynamic_slice_in_dim(modulated, start, own_block.shape[1], axis=1),
+            own_block,
+            preferred_element_type=jnp.float32,
+        ),
     ).astype(jnp.bfloat16)
     queries = projected[0]
     factor = 1.0 / math.sqrt(head_size)

time: 158 us -> 125 us (0.79)
  waiting for transfers between devices: 98.6 us -> 43.2 us
  blocking collectives: 26.1 us -> 45.3 us
  starting transfers between devices: 0.08 us -> 3.07 us
  other arithmetic: 5.73 us -> 7.53 us
    all_gather x1 -> x0, waiting for transfers between devices: 33.1 us -> none  [body(): lax.all_gather(qkv_weight, 'blk', axis=1, tiled=True)]
    all_gather x1, waiting for transfers between devices: 24.4 us -> 3.46 us  [collect(): gathered = lax.all_gather(own_part, ('seq', 'tp'), axis=1, tiled=True)]
    all_gather x1, blocking collectives: 14.8 us -> 33.4 us  [body(): lax.all_gather(out_weight, 'blk', axis=1, tiled=True)]
    ppermute x0 -> x1, starting transfers between devices: none -> 3.03 us  [product_in_turn(): upcoming = lax.ppermute(current, axis, right) if hop < size - 1 else None]
    convert_element_type x0 -> x1, other arithmetic: none -> 1.81 us  [body(): (normed * (1.0 + table_row[1]) + table_row[0]).astype(jnp.bfloat16)]
    dot_general x1 -> x2, matrix products: 3.52 us -> 1.98 us  [body(): jnp.einsum('td,kde->kte', lax.dynamic_slice_in_dim(modulated, start, own_...]
    unnamed x4 -> x3, waiting for transfers between devices: 41.1 us -> 39.8 us
    unnamed x4 -> x6, local copies, waits for them, and re-layouts: 4.33 us -> 4.34 us
  transfers between devices with their start and end apart: 3 -> 3, of which waited for: 3 -> 2; matrix products, arithmetic and copies ran while one was open for 3% -> 6% of each run, Pallas kernels for 0% -> 0%
where the time goes in v1:
time: 125 us
  blocking collectives  45.3 us (36%)
  waiting for transfers between devices  43.2 us (35%)
  between operations  14.8 us (12%)
  other arithmetic  7.53 us (6%)
  matrix products  5.51 us (4%)
  local copies, waits for them, and re-layouts  5.19 us (4%)
  starting transfers between devices  3.07 us (2%)
    unnamed x3, waiting for transfers between devices  39.8 us
    all_gather x1, blocking collectives, body(): lax.all_gather(out_weight, 'blk', axis=1, tiled=True)  33.4 us
    all_gather x1, blocking collectives, body(): key_piece = lax.all_gather(projected[1], 'blk', axis=0, tiled=True)  6.29 us
    all_gather x1, blocking collectives, body(): value_piece = lax.all_gather(projected[2], 'blk', axis=0, tiled=True)  5.62 us
    unnamed x6, local copies, waits for them, and re-layouts  4.34 us
    all_gather x1, waiting for transfers between devices, collect(): gathered = lax.all_gather(own_part, ('seq', 'tp'), axis=1, tiled=True)  3.46 us
    ppermute x1, starting transfers between devices, product_in_turn(): upcoming = lax.ppermute(current, axis, right) if hop < size - 1 else None  3.03 us
    reduce_sum x1, other arithmetic, body(): average = jnp.mean(gathered, axis=1, keepdims=True)  2.53 us
  transfers between devices with their start and end apart: 3, of which 2 were waited for; matrix products, arithmetic and copies ran while one was open for 6% of the time, Pallas kernels for 0%

profile of v1, /device:TPU:0, one launch (start us, length us, event | category | flops | bytes accessed | tf_op | source)
XLA Modules:
  0.0 124.7 jit_solution(224733968441123272)
XLA Ops:
  6.5 0.0 all-gather.4.cloned.1.call-start
  6.5 0.7 all-gather.4.cloned.1.call-update
  7.3 0.0 reduce-scatter.4.cloned.1.call-start
  7.3 3.0 %collective-permute-start = (bf16[3,1536,128]{2,1,0:T(8,128)(2,1)}, bf16[3,1536,128]{2,1,0:T(8,128)(2,1)S(1)}, u32[]{:S(2)}, u32[]{:S(2)}) collective-permute-start(bf16[3,1536,128]{2,1,0:T(8,128)(2,1)} %param.12), channel_id=1, source_target_pairs={{0,2},{2,0},{1,3},{3,1},{4,6},{6,4},{5,7},{7,5},{8,10},{10,8},{9,1... | collective-permute-start | bytes 3538952 | tf_op jit(solution)/shard_map/ppermute | solution.py:16
  11.7 33.4 %all_gather.15 = bf16[128,3072]{1,0:T(8,128)(2,1)} all-gather(bf16[128,1536]{1,0:T(8,128)(2,1)} %param.13), channel_id=1, replica_groups=mesh['group'=2,'seq'=4,'blk'=2,'tp'=2] {'blk'}, dimensions={1}, use_global_device_ids=true | all-gather | bytes 1179648 | tf_op jit(solution)/shard_map/all_gather | solution.py:94
  45.0 1.0 dynamic-slice_add_fusion
  46.0 3.5 %all-gather.4.cloned.1.call-done = bf16[512,3072]{1,0:T(8,128)(2,1)} async-done(((bf16[512,384]{1,0:T(8,128)(2,1)}), bf16[512,3072]{1,0:T(8,128)(2,1)}) %all-gather.4.cloned.1.call-update) | async-done | bytes 3145744 | tf_op jit(solution)/shard_map/all_gather | solution.py:24
  49.5 2.5 %convert_reduce_fusion = f32[512]{0:T(512)S(1)} fusion(bf16[512,3072]{1,0:T(8,128)(2,1)} %all-gather.4.cloned.1.call-done), kind=kLoop, calls=%fused_computation.16 | loop fusion | flops 3145216 | bytes 3147776 | tf_op jit(solution)/shard_map/reduce_sum | solution.py:56
  52.0 0.3 copy-done
  52.3 1.0 fusion.11
  53.3 0.0 copy-start.1
  53.3 1.8 %fusion.14 = bf16[512,3072]{1,0:T(8,128)(2,1)S(1)} fusion(bf16[512,3072]{1,0:T(8,128)(2,1)S(1)} %copy-done, f32[3072]{0:T(1024)S(1)} %bitcast.38, f32[3072]{0:T(1024)S(1)} %bitcast.37, f32[512]{0:T(512)S(1)} %add_rsqrt_fusion, f32[512]{0:T(512)S(1)} %broadcast_multiply_fusion), kind=kLoop, calls=%fused_computation.22 | loop fusion | flops 9437184 | bytes 6320128 | tf_op jit(solution)/shard_map/convert_element_type | solution.py:60
  55.1 0.0 copy-done.1
  55.1 1.0 fusion.17
  56.1 0.0 collective-permute-done
  56.1 1.0 fusion.27
  57.1 6.3 %all-gather = bf16[1,1024,128]{2,1,0:T(8,128)(2,1)S(1)} all-gather(bf16[1,512,128]{2,1,0:T(8,128)(2,1)S(1)} %get-tuple-element.178), channel_id=2, replica_groups=mesh['group'=2,'seq'=4,'blk'=2,'tp'=2] {'blk'}, dimensions={1}, use_global_device_ids=true | all-gather | bytes 393216 | tf_op jit(solution)/shard_map/all_gather | solution.py:79
  63.4 5.6 %all-gather.1 = bf16[1,1024,128]{2,1,0:T(8,128)(2,1)S(1)} all-gather(bf16[1,512,128]{2,1,0:T(8,128)(2,1)S(1)} %get-tuple-element.176), channel_id=3, replica_groups=mesh['group'=2,'seq'=4,'blk'=2,'tp'=2] {'blk'}, dimensions={1}, use_global_device_ids=true | all-gather | bytes 393216 | tf_op jit(solution)/shard_map/all_gather | solution.py:80
  69.1 1.9 %while.18 = (s32[]{:T(128)}, f32[512]{0:T(512)S(1)}, f32[512]{0:T(512)S(1)}, f32[512,128]{1,0:T(8,128)S(1)}, bf16[1024,128]{1,0:T(8,128)(2,1)S(1)}, /*index=5*/b...) while((s32[]{:T(128)}, f32[512]{0:T(512)S(1)}, ...), condition=%wide.region_5.6_spmd.clone, body=%wide.region_2.5_spmd.clone.sunk | while | flops 135989760 | bytes 4096175 | solution.py:88
  69.1 0.3 fusion.51
  69.4 0.2 fusion.52
  69.6 0.4 convolution_add_fusion.2
  70.0 0.3 fusion.51
  70.3 0.2 fusion.52
  70.6 0.4 convolution_add_fusion.2
  71.0 2.2 %convolution_convert_fusion = bf16[512,3072]{1,0:T(8,128)(2,1)S(1)} fusion(bf16[128,3072]{1,0:T(8,128)(2,1)} %all_gather.15, f32[512,128]{1,0:T(8,128)S(1)} %get-tuple-element.130, f32[512]{0:T(512)S(1)} %get-tuple-element.131, pred[]{:T(512)S(6)} %lt.41), kind=kOutput, calls=%fused_computation.23 | convolution fusion | flops 404422656 | bytes 4196353 | tf_op jit(solution)/shard_map/dot_general | solution.py:92
  73.1 2.8 %copy.7 = bf16[512,3072]{0,1:T(8,128)(2,1)} copy(bf16[512,3072]{1,0:T(8,128)(2,1)S(1)} %convolution_convert_fusion) | data formatting | bytes 6291456
  76.0 0.0 reduce-scatter.4.cloned.1.call-update
  76.0 0.8 dynamic-slice_reduce_fusion
  76.8 39.0 %reduce-scatter.4.cloned.1.call-done = bf16[384,512]{1,0:T(8,128)(2,1)} async-done(((bf16[3072,512]{1,0:T(8,128)(2,1)}), bf16[384,512]{1,0:T(8,128)(2,1)}) %reduce-scatter.4.cloned.1.call-update) | async-done | bytes 393232
  115.8 1.2 copy.8
  117.1 0.8 multiply_convert_fusion
  (13 shorter events, 0.1 us)
Async XLA Ops:
  6.5 42.9 %all-gather.4.cloned.1.call-start = ((), (), s32[]{:S(2)}) async-start(), calls=%async_computation.1 | async-start | bytes 3538944 | tf_op jit(solution)/shard_map/all_gather | solution.py:24
  7.3 108.6 %reduce-scatter.4.cloned.1.call-start = ((), (), s32[]{:S(2)}) async-start(), calls=%async_computation.2 | async-start | bytes 3538944
  7.3 48.8 %collective-permute-start = (bf16[3,1536,128]{2,1,0:T(8,128)(2,1)}, bf16[3,1536,128]{2,1,0:T(8,128)(2,1)S(1)}, u32[]{:S(2)}, u32[]{:S(2)}) collective-permute-start(bf16[3,1536,128]{2,1,0:T(8,128)(2,1)} %param.12), channel_id=1, source_target_pairs={{0,2},{2,0},{1,3},{3,1},{4,6},{6,4},{5,7},{7,5},{8,10},{10,8},{9,1... | collective-permute-start | bytes 3538952 | tf_op jit(solution)/shard_map/ppermute | solution.py:16
  49.5 2.8 %copy-start = (bf16[512,3072]{1,0:T(8,128)(2,1)S(1)}, bf16[512,3072]{1,0:T(8,128)(2,1)}, u32[]{:S(2)}) copy-start(bf16[512,3072]{1,0:T(8,128)(2,1)} %all-gather.4.cloned.1.call-done) | copy-start | bytes 9437188
  53.3 1.8 %copy-start.1 = (bf16[3,1536,128]{2,1,0:T(8,128)(2,1)S(1)}, bf16[3,1536,128]{2,1,0:T(8,128)(2,1)}, u32[]{:S(2)}) copy-start(bf16[3,1536,128]{2,1,0:T(8,128)(2,1)} %param.12) | copy-start | bytes 3538948
Sparse Core Ops, SparseCore 0:
  8.9 40.4 all-gather.3
  76.1 39.6 reduce-scatter.3
